TPU v7x, 128 devices: a whole 4x4x4 slice. The times are simulated.
128 devices in a mesh: tm: 16 (over y, x), orb: 8 (over z, core).
Axes of the slice: x: 4, y: 4, z: 4, core: 2. Of those that a mesh axis runs over, the one named last changes fastest.
Arguments:
- forward: bfloat16 [2, 2, 512, 128, 128], P(None, None, 'tm'), may hold values from -2 to 2
- backward_slab: bfloat16 [2, 2, 512, 128, 128], P(None, None, 'tm', 'orb'), may hold values from -2 to 2
- slot_time: int32 [512], replicated, may hold values from 0 to 511, as said below
- pattern: int32 [128, 128], replicated, may hold values 0 or 1
- coupling: float32 [128, 128], replicated, may hold values from -1 to 1
- hamiltonian: float32 [128, 128], replicated, may hold values from -0.8 to 0.8
- lesser_now: float32 [2, 128, 128], replicated, may hold values from -1.5 to 1.5
Outputs:
- lesser_next: float32 [2, 128, 128], P(None, 'orb')
Inputs may be any that keep to these rules, and one draw needn't show every extreme that they name: slot_time is a permutation of the 512 history times. The 32 slots of each index d of tm hold exactly 32 // 16 times of the range [e * 32, (e + 1) * 32) for every index e of tm.
All inputs are finite; a program needn't handle non-finite values.
Results may differ from a plain program's by a relative error of at most 0.0054.
Values may be sent and summed in bfloat16 or wider, within the bound.
No kernel may reach another device: no remote copies, remote signals or barrier semaphores. Data moves between devices by JAX's collectives and lax.ppermute only.
A program may use at most 64 MiB of HBM per device.

v0:
```python
import math
import jax
import jax.numpy as jnp
from jax import lax
from jax.sharding import PartitionSpec as P

history_step = 0.02
update_step = 0.5


def complex_einsum(form, left_re, left_im, right_re, right_im):
    real_part = jnp.einsum(
        form, left_re, right_re, preferred_element_type=jnp.float32
    ) - jnp.einsum(form, left_im, right_im, preferred_element_type=jnp.float32)
    imag_part = jnp.einsum(
        form, left_re, right_im, preferred_element_type=jnp.float32
    ) + jnp.einsum(form, left_im, right_re, preferred_element_type=jnp.float32)
    return (real_part, imag_part)


def self_energy(fwd_re, fwd_im, back_re, back_im, interaction, inter_rows, row_start, row_count):
    rows_re = lax.dynamic_slice_in_dim(fwd_re, row_start, row_count, 1)
    rows_im = lax.dynamic_slice_in_dim(fwd_im, row_start, row_count, 1)
    fwd_re32 = fwd_re.astype(jnp.float32)
    fwd_im32 = fwd_im.astype(jnp.float32)
    trans_re = jnp.swapaxes(back_re, 1, 2).astype(jnp.float32)
    trans_im = jnp.swapaxes(back_im, 1, 2).astype(jnp.float32)
    bubble_re = (fwd_re32 * trans_re - fwd_im32 * trans_im).astype(jnp.bfloat16)
    bubble_im = (fwd_re32 * trans_im + fwd_im32 * trans_re).astype(jnp.bfloat16)
    left_re = jnp.einsum(
        "ik,skj->sij", inter_rows, bubble_re, preferred_element_type=jnp.float32
    ).astype(jnp.bfloat16)
    left_im = jnp.einsum(
        "ik,skj->sij", inter_rows, bubble_im, preferred_element_type=jnp.float32
    ).astype(jnp.bfloat16)
    screen_re = jnp.einsum("sik,kj->sij", left_re, interaction, preferred_element_type=jnp.float32)
    screen_im = jnp.einsum("sik,kj->sij", left_im, interaction, preferred_element_type=jnp.float32)
    rows_re32 = rows_re.astype(jnp.float32)
    rows_im32 = rows_im.astype(jnp.float32)
    direct_re = rows_re32 * screen_re - rows_im32 * screen_im
    direct_im = rows_re32 * screen_im + rows_im32 * screen_re
    inter_rows32 = inter_rows.astype(jnp.float32)
    scaled_re = (inter_rows32[None, :, :, None] * fwd_re32[:, None]).astype(jnp.bfloat16)
    scaled_im = (inter_rows32[None, :, :, None] * fwd_im32[:, None]).astype(jnp.bfloat16)
    inner_re, inner_im = complex_einsum("slm,simj->silj", back_re, back_im, scaled_re, scaled_im)
    inter32 = interaction.astype(jnp.float32)
    weighted_re = (inner_re * inter32).astype(jnp.bfloat16)
    weighted_im = (inner_im * inter32).astype(jnp.bfloat16)
    exch_re, exch_im = complex_einsum("sil,silj->sij", rows_re, rows_im, weighted_re, weighted_im)
    sigma_re = (direct_re - exch_re).astype(jnp.bfloat16)
    sigma_im = (direct_im - exch_im).astype(jnp.bfloat16)
    return (sigma_re, sigma_im)


def block_terms(fwd_block, back_block, weights, interaction, inter_rows, row_start, row_count):
    summed = None
    scale = weights[:, None, None]
    for branch in (0, 1):
        other = 1 - branch
        factor = 1.0 if branch == 0 else -1.0
        sigma_re, sigma_im = self_energy(
            fwd_block[branch, 0],
            fwd_block[branch, 1],
            back_block[other, 0],
            back_block[other, 1],
            interaction,
            inter_rows,
            row_start,
            row_count,
        )
        prod_re, prod_im = complex_einsum(
            "sil,slj->sij", sigma_re, sigma_im, back_block[other, 0], back_block[other, 1]
        )
        term = factor * jnp.stack(
            [jnp.sum(scale * prod_re, axis=0), jnp.sum(scale * prod_im, axis=0)]
        )
        summed = term if summed is None else summed + term
    return summed


def history_terms(fwd_part, back_part, weights, interaction, inter_rows, row_start, row_count):
    slices_here = fwd_part.shape[2]
    block_size = math.gcd(max(4, 128 // row_count), slices_here)
    block_count = slices_here // block_size
    orbitals = fwd_part.shape[3]

    def add_block(block, running):
        start = block * block_size
        fwd_block = lax.dynamic_slice_in_dim(fwd_part, start, block_size, 2)
        back_block = lax.dynamic_slice_in_dim(back_part, start, block_size, 2)
        weight_block = lax.dynamic_slice_in_dim(weights, start, block_size, 0)
        return running + block_terms(
            fwd_block, back_block, weight_block, interaction, inter_rows, row_start, row_count
        )

    initial = jnp.zeros((2, row_count, orbitals), jnp.float32)
    return lax.fori_loop(0, block_count, add_block, initial)


def on_device(forward, backward_slab, slot_time, pattern, coupling, hamiltonian, lesser_now):
    tm_count = lax.axis_size("tm")
    my_time = lax.axis_index("tm")
    my_orb = lax.axis_index("orb")
    per_device = forward.shape[2]
    row_count = backward_slab.shape[3]
    per_peer = per_device // tm_count
    slices_all = per_device * tm_count
    row_start = my_orb * row_count
    time_start = my_time * per_device
    holder_of = slot_time // per_device
    my_holders = lax.dynamic_slice_in_dim(holder_of, time_start, per_device)
    send_order = jnp.argsort(my_holders, stable=True)
    sorted_slab = jnp.take(backward_slab, send_order, axis=2)
    holder_grid = holder_of.reshape(tm_count, per_device)
    time_grid = slot_time.reshape(tm_count, per_device)
    not_mine = (holder_grid != my_time).astype(jnp.int32)
    positions = jnp.argsort(not_mine, axis=1, stable=True)[:, :per_peer]
    times_here = jnp.take_along_axis(time_grid, positions, axis=1).reshape(per_device)
    natural = jnp.argsort(times_here - time_start)
    masked = coupling * pattern.astype(jnp.float32)
    interaction = ((masked + masked.T) * 0.5).astype(jnp.bfloat16)
    inter_rows = lax.dynamic_slice_in_dim(interaction, row_start, row_count, 0)
    time_index = time_start + jnp.arange(per_device, dtype=jnp.int32)
    edges = (time_index == 0) | (time_index == slices_all - 1)
    weights = jnp.where(edges, jnp.float32(0.5), jnp.float32(1.0)) * history_step
    full_sorted = lax.all_gather(sorted_slab, "orb", axis=3, tiled=True)
    arrived = lax.all_to_all(full_sorted, "tm", split_axis=2, concat_axis=2, tiled=True)
    back_full = jnp.take(arrived, natural, axis=2)
    local_collision = history_terms(
        forward, back_full, weights, interaction, inter_rows, row_start, row_count
    )
    summed_rows = lax.psum(local_collision, "tm")
    collision = lax.all_gather(summed_rows, "orb", axis=1, tiled=True)
    own_rows = lax.dynamic_slice_in_dim(collision, row_start, row_count, 1)
    own_columns = lax.dynamic_slice_in_dim(collision, row_start, row_count, 2)
    herm_re = own_rows[0] + own_columns[0].T
    herm_im = own_rows[1] - own_columns[1].T
    high = lax.Precision.HIGHEST
    ham_rows = lax.dynamic_slice_in_dim(hamiltonian, row_start, row_count, 0)
    lesser_rows = lax.dynamic_slice_in_dim(lesser_now, row_start, row_count, 1)
    comm_re = jnp.dot(ham_rows, lesser_now[0], precision=high) - jnp.dot(
        lesser_rows[0], hamiltonian, precision=high
    )
    comm_im = jnp.dot(ham_rows, lesser_now[1], precision=high) - jnp.dot(
        lesser_rows[1], hamiltonian, precision=high
    )
    next_re = lesser_rows[0] + update_step * (comm_im + herm_im)
    next_im = lesser_rows[1] - update_step * (comm_re + herm_re)
    return jnp.stack([next_re, next_im])


def solution(mesh):
    in_specs = (
        P(None, None, "tm", None, None),
        P(None, None, "tm", "orb", None),
        P(),
        P(),
        P(),
        P(),
        P(),
    )
    out_specs = P(None, "orb", None)
    return jax.shard_map(
        on_device, mesh=mesh, in_specs=in_specs, out_specs=out_specs, check_vma=False
    )
```

profile of v0, /device:TPU:1, one launch (start us, length us, event | category | flops | bytes accessed | tf_op | source)
XLA Modules:
  0.0 479.0 jit_solution(11907473625283810762)
XLA Ops:
  10.6 39.5 %all-gather.2.cloned.1.call-done = bf16[2,2,32,128,128]{4,3,1,0,2:T(8,128)(2,1)} async-done(((bf16[2,2,32,16,128]{4,3,1,0,2:T(8,128)(2,1)}), bf16[2,2,32,128,128]{4,3,1,0,2:T(8,128)(2,1)}) %all-gather.2.cloned.1.call-update) | async-done | bytes 4194320 | tf_op jit(solution)/shard_map/all_gather | solution.py:126
  50.1 6.6 %all-to-all-start = ((bf16[2,2,32,128,128]{4,3,1,0,2:T(8,128)(2,1)}), bf16[2,2,32,128,128]{4,3,1,0,2:T(8,128)(2,1)}, u32[]{:S(2)}, u32[]{:S(2)}) async-start(bf16[2,2,32,128,128]{4,3,1,0,2:T(8,128)(2,1)} %all-gather.2.cloned.1.call-done), calls=%async_computation | async-start | bytes 8388608 | tf_op jit(solution)/shard_map/all_to_all | solution.py:127
  64.0 55.6 %all-to-all-done = bf16[2,2,32,128,128]{4,3,1,0,2:T(8,128)(2,1)} async-done(((bf16[2,2,32,128,128]{4,3,1,0,2:T(8,128)(2,1)}), bf16[2,2,32,128,128]{4,3,1,0,2:T(8,128)(2,1)}, u32[]{:S(2)}, u32[]{:S(2)}) %all-to-all-start) | async-done | bytes 4194336 | tf_op jit(solution)/shard_map/all_to_all | solution.py:127
  119.6 4.7 copy.45
  124.3 5.2 %gather_fusion.1 = bf16[32,2,2,128,128]{4,3,2,1,0:T(8,128)(2,1)} fusion(bf16[2,2,32,128,128]{4,3,2,1,0:T(8,128)(2,1)} %copy.45, s32[1024]{0:T(1024)S(1)} %pad_clamp_fusion), kind=kCustom, calls=%fused_computation.1 | custom fusion | bytes 8388736 | tf_op jit(solution)/shard_map/jit(_take)/gather | solution.py:128
  129.5 4.6 select_bitcast_fusion
  134.1 249.0 %while.16 = (s32[]{:T(128)}, f32[2,16,128]{2,1,0:T(8,128)}, f32[32]{0:T(128)S(1)}, bf16[2,2,32,128,128]{4,3,2,1,0:T(8,128)(2,1)}, s32[]{:T(128)}, /*index=5*/bf1...) while((s32[]{:T(128)}, f32[2,16,128]{2,1,0:T(8,128)}, ...), condition=%wide.region_8.9_spmd.clone, body=%wide.region_3.8_spmd.clone.sunk | while | flops 4459808768 | bytes 142112496 | solution.py:97
  148.4 2.6 fusion.413
  153.3 2.3 fusion.414
  157.8 2.6 fusion.410
  162.7 2.3 fusion.411
  173.2 2.6 fusion.427
  178.1 2.3 fusion.428
  182.5 2.6 fusion.424
  187.5 2.3 fusion.425
  210.6 2.6 fusion.413
  215.5 2.3 fusion.414
  220.0 2.6 fusion.410
  224.9 2.3 fusion.411
  235.4 2.6 fusion.427
  240.3 2.3 fusion.428
  244.8 2.6 fusion.424
  272.9 2.6 fusion.413
  282.3 2.6 fusion.410
  297.6 2.6 fusion.427
  307.0 2.6 fusion.424
  335.1 2.6 fusion.413
  344.5 2.6 fusion.410
  359.9 2.6 fusion.427
  369.3 2.6 fusion.424
  383.1 58.1 %psum.7 = f32[2,16,128]{2,1,0:T(8,128)S(1)} all-reduce(f32[2,16,128]{2,1,0:T(8,128)} %get-tuple-element.204), channel_id=1, replica_groups=mesh['tm'=16,'orb'=8] {'tm'}, use_global_device_ids=true, to_apply=%region_9.10 | all-reduce | flops 4096 | bytes 32768 | tf_op jit(solution)/shard_map/psum | solution.py:132
  441.1 28.1 %all_gather.7 = f32[2,128,128]{2,1,0:T(8,128)S(1)} all-gather(f32[2,16,128]{2,1,0:T(8,128)S(1)} %psum.7), channel_id=1, replica_groups=mesh['tm'=16,'orb'=8] {'orb'}, dimensions={1}, use_global_device_ids=true | all-gather | bytes 147456 | tf_op jit(solution)/shard_map/all_gather | solution.py:133
  (287 shorter events, 204.2 us)
Async XLA Ops:
  6.5 2.5 copy-start
  6.5 43.6 %all-gather.2.cloned.1.call-start = ((), (), s32[]{:S(2)}) async-start(), calls=%async_computation.1 | async-start | bytes 4718592 | tf_op jit(solution)/shard_map/all_gather | solution.py:126
  10.6 46.1 %copy-start.11 = (s32[512]{0:T(512)S(1)}, s32[512]{0:T(512)}, u32[]{:S(2)}) copy-start(s32[512]{0:T(512)} %param.11) | copy-start | bytes 6148
  50.1 69.5 %all-to-all-start = ((bf16[2,2,32,128,128]{4,3,1,0,2:T(8,128)(2,1)}), bf16[2,2,32,128,128]{4,3,1,0,2:T(8,128)(2,1)}, u32[]{:S(2)}, u32[]{:S(2)}) async-start(bf16[2,2,32,128,128]{4,3,1,0,2:T(8,128)(2,1)} %all-gather.2.cloned.1.call-done), calls=%async_computation | async-start | bytes 8388608 | tf_op jit(solution)/shard_map/all_to_all | solution.py:127
  57.9 1.1 copy-start.9
  58.0 1.2 copy-start.10
  58.0 3.1 copy-start.8
  134.1 6.7 %copy-start.2 = (bf16[128,128]{1,0:T(8,128)(2,1)}, bf16[128,128]{1,0:T(8,128)(2,1)S(1)}, u32[]{:S(2)}) copy-start(bf16[128,128]{1,0:T(8,128)(2,1)S(1)} %get-tuple-element.394) | copy-start | bytes 98308 | tf_op jit(solution)/shard_map/while
  160.4 4.5 copy-start.5
  185.2 4.5 copy-start.3
  185.2 4.5 copy-start.4
  187.5 8.3 %copy-start.6 = (f32[2,16,128]{2,1,0:T(8,128)S(1)}, f32[2,16,128]{2,1,0:T(8,128)}, u32[]{:S(2)}) copy-start(f32[2,16,128]{2,1,0:T(8,128)} %get-tuple-element.375) | copy-start | bytes 49156 | tf_op jit(solution)/shard_map/while
  187.5 8.9 %copy-start.13 = (f32[32]{0:T(128)S(1)}, f32[32]{0:T(128)}, u32[]{:S(2)}) copy-start(f32[32]{0:T(128)} %copy-done.12) | copy-start | bytes 388 | tf_op jit(solution)/shard_map/while
  196.4 6.7 %copy-start.2 = (bf16[128,128]{1,0:T(8,128)(2,1)}, bf16[128,128]{1,0:T(8,128)(2,1)S(1)}, u32[]{:S(2)}) copy-start(bf16[128,128]{1,0:T(8,128)(2,1)S(1)} %get-tuple-element.394) | copy-start | bytes 98308 | tf_op jit(solution)/shard_map/while
  222.7 4.5 copy-start.5
  247.4 4.5 copy-start.3
  247.4 4.5 copy-start.4
  249.7 8.3 %copy-start.6 = (f32[2,16,128]{2,1,0:T(8,128)S(1)}, f32[2,16,128]{2,1,0:T(8,128)}, u32[]{:S(2)}) copy-start(f32[2,16,128]{2,1,0:T(8,128)} %get-tuple-element.375) | copy-start | bytes 49156 | tf_op jit(solution)/shard_map/while
  249.7 8.9 %copy-start.13 = (f32[32]{0:T(128)S(1)}, f32[32]{0:T(128)}, u32[]{:S(2)}) copy-start(f32[32]{0:T(128)} %copy-done.12) | copy-start | bytes 388 | tf_op jit(solution)/shard_map/while
  258.6 6.7 %copy-start.2 = (bf16[128,128]{1,0:T(8,128)(2,1)}, bf16[128,128]{1,0:T(8,128)(2,1)S(1)}, u32[]{:S(2)}) copy-start(bf16[128,128]{1,0:T(8,128)(2,1)S(1)} %get-tuple-element.394) | copy-start | bytes 98308 | tf_op jit(solution)/shard_map/while
  284.9 4.5 copy-start.5
  309.7 4.5 copy-start.3
  309.7 4.5 copy-start.4
  311.9 8.3 %copy-start.6 = (f32[2,16,128]{2,1,0:T(8,128)S(1)}, f32[2,16,128]{2,1,0:T(8,128)}, u32[]{:S(2)}) copy-start(f32[2,16,128]{2,1,0:T(8,128)} %get-tuple-element.375) | copy-start | bytes 49156 | tf_op jit(solution)/shard_map/while
  311.9 8.9 %copy-start.13 = (f32[32]{0:T(128)S(1)}, f32[32]{0:T(128)}, u32[]{:S(2)}) copy-start(f32[32]{0:T(128)} %copy-done.12) | copy-start | bytes 388 | tf_op jit(solution)/shard_map/while
  320.8 6.7 %copy-start.2 = (bf16[128,128]{1,0:T(8,128)(2,1)}, bf16[128,128]{1,0:T(8,128)(2,1)S(1)}, u32[]{:S(2)}) copy-start(bf16[128,128]{1,0:T(8,128)(2,1)S(1)} %get-tuple-element.394) | copy-start | bytes 98308 | tf_op jit(solution)/shard_map/while
  347.1 4.5 copy-start.5
  371.9 4.5 copy-start.3
  371.9 4.5 copy-start.4
  374.2 8.3 %copy-start.6 = (f32[2,16,128]{2,1,0:T(8,128)S(1)}, f32[2,16,128]{2,1,0:T(8,128)}, u32[]{:S(2)}) copy-start(f32[2,16,128]{2,1,0:T(8,128)} %get-tuple-element.375) | copy-start | bytes 49156 | tf_op jit(solution)/shard_map/while
  374.2 8.9 %copy-start.13 = (f32[32]{0:T(128)S(1)}, f32[32]{0:T(128)}, u32[]{:S(2)}) copy-start(f32[32]{0:T(128)} %copy-done.12) | copy-start | bytes 388 | tf_op jit(solution)/shard_map/while
  383.1 89.1 %copy-start.1 = (bf16[2,2,32,16,128]{4,3,2,1,0:T(8,128)(2,1)S(1)}, bf16[2,2,32,16,128]{4,3,2,1,0:T(8,128)(2,1)}, u32[]{:S(2)}) copy-start(bf16[2,2,32,16,128]{4,3,2,1,0:T(8,128)(2,1)} %param.10) | copy-start | bytes 1572868
  (8 other events, 4.4 us)
Sparse Core Ops, SparseCore 0:
  10.7 39.3 all-gather.1
where the time goes:
time: 482 us; the launch traced here: 479 us
  matrix products  219 us (45%)
  waiting for transfers between devices  95.1 us (20%)
  blocking collectives  86.2 us (18%)
  local copies, waits for them, and re-layouts  46.3 us (10%)
  between operations  13.6 us (3%)
  other arithmetic  11.6 us (2%)
  starting transfers between devices  6.58 us (1%)
    psum x1, blocking collectives, on_device(): summed_rows = lax.psum(local_collision, 'tm')  58.1 us
    all_to_all x1, waiting for transfers between devices, on_device(): lax.all_to_all(full_sorted, 'tm', split_axis=2, concat_axis=2, tiled=True)  55.6 us
    dot_general x24, matrix products, complex_einsum(): jnp.einsum(form, left_re, right_im, preferred_element_type=jnp.float32)  48.3 us
    dot_general x24, matrix products, complex_einsum(): jnp.einsum(form, left_im, right_im, preferred_element_type=jnp.float32)  48.2 us
    dot_general x24, matrix products, complex_einsum(): jnp.einsum(form, left_im, right_re, preferred_element_type=jnp.float32)  45 us
    dot_general x24, matrix products, complex_einsum(): jnp.einsum(form, left_re, right_re, preferred_element_type=jnp.float32)  44.8 us
    all_gather x1, waiting for transfers between devices, on_device(): full_sorted = lax.all_gather(sorted_slab, 'orb', axis=3, tiled=True)  39.5 us
    all_gather x1, blocking collectives, on_device(): collision = lax.all_gather(summed_rows, 'orb', axis=1, tiled=True)  28.1 us
  transfers between devices with their start and end apart: 2, of which 2 were waited for; matrix products, arithmetic and copies ran while one was open for 1% of the time, Pallas kernels for 0%

commit v1 on v0

--- a/solution.py
+++ b/solution.py
@@ -129,7 +129,11 @@
     local_collision = history_terms(
         forward, back_full, weights, interaction, inter_rows, row_start, row_count
     )
-    summed_rows = lax.psum(local_collision, "tm")
+    summed_rows = local_collision
+    for hop in (1, 2, 4, 8):
+        summed_rows = summed_rows + lax.ppermute(
+            summed_rows, "tm", [(dev, dev ^ hop) for dev in range(16)]
+        )
     collision = lax.all_gather(summed_rows, "orb", axis=1, tiled=True)
     own_rows = lax.dynamic_slice_in_dim(collision, row_start, row_count, 1)
     own_columns = lax.dynamic_slice_in_dim(collision, row_start, row_count, 2)

time: 482 us -> 428 us (0.89)
  blocking collectives: 86.2 us -> 18.3 us
  waiting for transfers between devices: 95.1 us -> 105 us
    psum x1 -> x0, blocking collectives: 58.1 us -> none  [on_device(): summed_rows = lax.psum(local_collision, 'tm')]
    all_gather x1, blocking collectives: 28.1 us -> 18.3 us  [on_device(): collision = lax.all_gather(summed_rows, 'orb', axis=1, tiled=True)]
    ppermute x0 -> x4, waiting for transfers between devices: none -> 7.44 us  [on_device(): lax.ppermute(summed_rows, 'tm', [(dev, dev ^ hop) for dev in range(16)])]
  transfers between devices with their start and end apart: 2 -> 6, of which waited for: 2 -> 6; matrix products, arithmetic and copies ran while one was open for 1% -> 2% of each run, Pallas kernels for 0% -> 0%
where the time goes in v1:
time: 428 us; the launch traced here: 424 us
  matrix products  218 us (51%)
  waiting for transfers between devices  105 us (25%)
  local copies, waits for them, and re-layouts  46.3 us (11%)
  blocking collectives  18.3 us (4%)
  between operations  13.6 us (3%)
  other arithmetic  13.1 us (3%)
  starting transfers between devices  8.91 us (2%)
    all_to_all x1, waiting for transfers between devices, on_device(): lax.all_to_all(full_sorted, 'tm', split_axis=2, concat_axis=2, tiled=True)  58.5 us
    dot_general x24, matrix products, complex_einsum(): jnp.einsum(form, left_re, right_im, preferred_element_type=jnp.float32)  48.3 us
    dot_general x24, matrix products, complex_einsum(): jnp.einsum(form, left_im, right_im, preferred_element_type=jnp.float32)  48.2 us
    dot_general x24, matrix products, complex_einsum(): jnp.einsum(form, left_im, right_re, preferred_element_type=jnp.float32)  45 us
    dot_general x24, matrix products, complex_einsum(): jnp.einsum(form, left_re, right_re, preferred_element_type=jnp.float32)  44.8 us
    all_gather x1, waiting for transfers between devices, on_device(): full_sorted = lax.all_gather(sorted_slab, 'orb', axis=3, tiled=True)  39.5 us
    all_gather x1, blocking collectives, on_device(): collision = lax.all_gather(summed_rows, 'orb', axis=1, tiled=True)  18.3 us
    dot_general x8, matrix products, self_energy(): jnp.einsum('sik,kj->sij', left_re, interaction, preferred_element_type=jn...  16.2 us
  transfers between devices with their start and end apart: 6, of which 6 were waited for; matrix products, arithmetic and copies ran while one was open for 2% of the time, Pallas kernels for 0%

profile of v1, /device:TPU:1, one launch (start us, length us, event | category | flops | bytes accessed | tf_op | source)
XLA Modules:
  0.0 424.4 jit_solution(10098816386899053415)
XLA Ops:
  10.6 39.5 %all-gather.2.cloned.1.call-done = bf16[2,2,32,128,128]{4,3,1,0,2:T(8,128)(2,1)} async-done(((bf16[2,2,32,16,128]{4,3,1,0,2:T(8,128)(2,1)}), bf16[2,2,32,128,128]{4,3,1,0,2:T(8,128)(2,1)}) %all-gather.2.cloned.1.call-update) | async-done | bytes 4194320 | tf_op jit(solution)/shard_map/all_gather | solution.py:126
  50.1 6.6 %all-to-all-start = ((bf16[2,2,32,128,128]{4,3,1,0,2:T(8,128)(2,1)}), bf16[2,2,32,128,128]{4,3,1,0,2:T(8,128)(2,1)}, u32[]{:S(2)}, u32[]{:S(2)}) async-start(bf16[2,2,32,128,128]{4,3,1,0,2:T(8,128)(2,1)} %all-gather.2.cloned.1.call-done), calls=%async_computation | async-start | bytes 8388608 | tf_op jit(solution)/shard_map/all_to_all | solution.py:127
  61.1 58.5 %all-to-all-done = bf16[2,2,32,128,128]{4,3,1,0,2:T(8,128)(2,1)} async-done(((bf16[2,2,32,128,128]{4,3,1,0,2:T(8,128)(2,1)}), bf16[2,2,32,128,128]{4,3,1,0,2:T(8,128)(2,1)}, u32[]{:S(2)}, u32[]{:S(2)}) %all-to-all-start) | async-done | bytes 4194336 | tf_op jit(solution)/shard_map/all_to_all | solution.py:127
  119.6 4.7 %copy.45 = bf16[2,2,32,128,128]{4,3,2,1,0:T(8,128)(2,1)} copy(bf16[2,2,32,128,128]{4,3,1,0,2:T(8,128)(2,1)} %all-to-all-done) | data formatting | bytes 8388608 | tf_op jit(solution)/shard_map/all_to_all | solution.py:127
  124.3 5.2 %gather_fusion.1 = bf16[32,2,2,128,128]{4,3,2,1,0:T(8,128)(2,1)} fusion(bf16[2,2,32,128,128]{4,3,2,1,0:T(8,128)(2,1)} %copy.45, s32[1024]{0:T(1024)S(1)} %pad_clamp_fusion), kind=kCustom, calls=%fused_computation.1 | custom fusion | bytes 8388736 | tf_op jit(solution)/shard_map/jit(_take)/gather | solution.py:128
  129.5 4.6 %select_bitcast_fusion = bf16[2,2,32,128,128]{4,3,1,0,2:T(8,128)(2,1)} fusion(bf16[32,2,2,128,128]{4,3,2,1,0:T(8,128)(2,1)} %gather_fusion.1, pred[32]{0:T(512)(128)(4,1)S(1)} %compare_and_fusion.1), kind=kLoop, calls=%fused_computation.226 | loop fusion | flops 2097152 | bytes 8388640 | tf_op jit(solution)/shard_map/jit(_take)/select_n | solution.py:128
  134.1 249.0 %while.16 = (s32[]{:T(128)}, f32[2,16,128]{2,1,0:T(8,128)}, f32[32]{0:T(128)S(1)}, bf16[2,2,32,128,128]{4,3,2,1,0:T(8,128)(2,1)}, s32[]{:T(128)}, /*index=5*/bf1...) while((s32[]{:T(128)}, f32[2,16,128]{2,1,0:T(8,128)}, ...), condition=%wide.region_8.9_spmd.clone, body=%wide.region_3.8_spmd.clone.sunk | while | flops 4459808768 | bytes 142112496 | solution.py:97
  148.4 2.6 fusion.413
  153.3 2.3 fusion.414
  157.8 2.6 fusion.410
  162.7 2.3 fusion.411
  173.2 2.6 fusion.427
  178.1 2.3 fusion.428
  182.5 2.6 fusion.424
  187.5 2.3 fusion.425
  210.6 2.6 fusion.413
  215.5 2.3 fusion.414
  220.0 2.6 fusion.410
  224.9 2.3 fusion.411
  235.4 2.6 fusion.427
  240.3 2.3 fusion.428
  244.8 2.6 fusion.424
  272.9 2.6 fusion.413
  282.3 2.6 fusion.410
  297.6 2.6 fusion.427
  307.0 2.6 fusion.424
  335.1 2.6 fusion.413
  344.5 2.6 fusion.410
  359.9 2.6 fusion.427
  369.3 2.6 fusion.424
  388.3 2.4 collective-permute-done.1
  397.7 18.3 %all_gather.7 = f32[2,128,128]{2,1,0:T(8,128)S(1)} all-gather(f32[2,16,128]{2,1,0:T(8,128)S(1)} %add.230), channel_id=1, replica_groups=mesh['tm'=16,'orb'=8] {'orb'}, dimensions={1}, use_global_device_ids=true | all-gather | bytes 147456 | tf_op jit(solution)/shard_map/all_gather | solution.py:137
  (297 shorter events, 212.2 us)
Async XLA Ops:
  6.5 43.6 %all-gather.2.cloned.1.call-start = ((), (), s32[]{:S(2)}) async-start(), calls=%async_computation.1 | async-start | bytes 4718592 | tf_op jit(solution)/shard_map/all_gather | solution.py:126
  10.6 46.1 %copy-start.10 = (s32[512]{0:T(512)S(1)}, s32[512]{0:T(512)}, u32[]{:S(2)}) copy-start(s32[512]{0:T(512)} %param.11) | copy-start | bytes 6148
  50.1 69.5 %all-to-all-start = ((bf16[2,2,32,128,128]{4,3,1,0,2:T(8,128)(2,1)}), bf16[2,2,32,128,128]{4,3,1,0,2:T(8,128)(2,1)}, u32[]{:S(2)}, u32[]{:S(2)}) async-start(bf16[2,2,32,128,128]{4,3,1,0,2:T(8,128)(2,1)} %all-gather.2.cloned.1.call-done), calls=%async_computation | async-start | bytes 8388608 | tf_op jit(solution)/shard_map/all_to_all | solution.py:127
  134.1 6.7 %copy-start.2 = (bf16[128,128]{1,0:T(8,128)(2,1)}, bf16[128,128]{1,0:T(8,128)(2,1)S(1)}, u32[]{:S(2)}) copy-start(bf16[128,128]{1,0:T(8,128)(2,1)S(1)} %get-tuple-element.396) | copy-start | bytes 98308 | tf_op jit(solution)/shard_map/while
  160.4 4.5 %copy-start.5 = (f32[8,16,128]{2,1,0:T(8,128)S(1)}, f32[8,16,128]{2,1,0:T(8,128)}, u32[]{:S(2)}) copy-start(f32[8,16,128]{2,1,0:T(8,128)} %fusion.408) | copy-start | bytes 196612 | tf_op jit(solution)/shard_map/while
  185.2 4.5 %copy-start.3 = (bf16[128,128]{1,0:T(8,128)(2,1)S(1)}, bf16[128,128]{1,0:T(8,128)(2,1)}, u32[]{:S(2)}) copy-start(bf16[128,128]{1,0:T(8,128)(2,1)} %copy-done.2) | copy-start | bytes 98308 | tf_op jit(solution)/shard_map/while
  185.2 4.5 %copy-start.4 = (f32[8,16,128]{2,1,0:T(8,128)S(1)}, f32[8,16,128]{2,1,0:T(8,128)}, u32[]{:S(2)}) copy-start(f32[8,16,128]{2,1,0:T(8,128)} %fusion.422) | copy-start | bytes 196612 | tf_op jit(solution)/shard_map/while
  187.5 8.3 %copy-start.6 = (f32[2,16,128]{2,1,0:T(8,128)S(1)}, f32[2,16,128]{2,1,0:T(8,128)}, u32[]{:S(2)}) copy-start(f32[2,16,128]{2,1,0:T(8,128)} %get-tuple-element.377) | copy-start | bytes 49156 | tf_op jit(solution)/shard_map/while
  187.5 8.9 %copy-start.12 = (f32[32]{0:T(128)S(1)}, f32[32]{0:T(128)}, u32[]{:S(2)}) copy-start(f32[32]{0:T(128)} %copy-done.11) | copy-start | bytes 388 | tf_op jit(solution)/shard_map/while
  196.4 6.7 %copy-start.2 = (bf16[128,128]{1,0:T(8,128)(2,1)}, bf16[128,128]{1,0:T(8,128)(2,1)S(1)}, u32[]{:S(2)}) copy-start(bf16[128,128]{1,0:T(8,128)(2,1)S(1)} %get-tuple-element.396) | copy-start | bytes 98308 | tf_op jit(solution)/shard_map/while
  222.7 4.5 %copy-start.5 = (f32[8,16,128]{2,1,0:T(8,128)S(1)}, f32[8,16,128]{2,1,0:T(8,128)}, u32[]{:S(2)}) copy-start(f32[8,16,128]{2,1,0:T(8,128)} %fusion.408) | copy-start | bytes 196612 | tf_op jit(solution)/shard_map/while
  247.4 4.5 %copy-start.3 = (bf16[128,128]{1,0:T(8,128)(2,1)S(1)}, bf16[128,128]{1,0:T(8,128)(2,1)}, u32[]{:S(2)}) copy-start(bf16[128,128]{1,0:T(8,128)(2,1)} %copy-done.2) | copy-start | bytes 98308 | tf_op jit(solution)/shard_map/while
  247.4 4.5 %copy-start.4 = (f32[8,16,128]{2,1,0:T(8,128)S(1)}, f32[8,16,128]{2,1,0:T(8,128)}, u32[]{:S(2)}) copy-start(f32[8,16,128]{2,1,0:T(8,128)} %fusion.422) | copy-start | bytes 196612 | tf_op jit(solution)/shard_map/while
  249.7 8.3 %copy-start.6 = (f32[2,16,128]{2,1,0:T(8,128)S(1)}, f32[2,16,128]{2,1,0:T(8,128)}, u32[]{:S(2)}) copy-start(f32[2,16,128]{2,1,0:T(8,128)} %get-tuple-element.377) | copy-start | bytes 49156 | tf_op jit(solution)/shard_map/while
  249.7 8.9 %copy-start.12 = (f32[32]{0:T(128)S(1)}, f32[32]{0:T(128)}, u32[]{:S(2)}) copy-start(f32[32]{0:T(128)} %copy-done.11) | copy-start | bytes 388 | tf_op jit(solution)/shard_map/while
  258.6 6.7 %copy-start.2 = (bf16[128,128]{1,0:T(8,128)(2,1)}, bf16[128,128]{1,0:T(8,128)(2,1)S(1)}, u32[]{:S(2)}) copy-start(bf16[128,128]{1,0:T(8,128)(2,1)S(1)} %get-tuple-element.396) | copy-start | bytes 98308 | tf_op jit(solution)/shard_map/while
  284.9 4.5 %copy-start.5 = (f32[8,16,128]{2,1,0:T(8,128)S(1)}, f32[8,16,128]{2,1,0:T(8,128)}, u32[]{:S(2)}) copy-start(f32[8,16,128]{2,1,0:T(8,128)} %fusion.408) | copy-start | bytes 196612 | tf_op jit(solution)/shard_map/while
  309.7 4.5 %copy-start.3 = (bf16[128,128]{1,0:T(8,128)(2,1)S(1)}, bf16[128,128]{1,0:T(8,128)(2,1)}, u32[]{:S(2)}) copy-start(bf16[128,128]{1,0:T(8,128)(2,1)} %copy-done.2) | copy-start | bytes 98308 | tf_op jit(solution)/shard_map/while
  309.7 4.5 %copy-start.4 = (f32[8,16,128]{2,1,0:T(8,128)S(1)}, f32[8,16,128]{2,1,0:T(8,128)}, u32[]{:S(2)}) copy-start(f32[8,16,128]{2,1,0:T(8,128)} %fusion.422) | copy-start | bytes 196612 | tf_op jit(solution)/shard_map/while
  311.9 8.3 %copy-start.6 = (f32[2,16,128]{2,1,0:T(8,128)S(1)}, f32[2,16,128]{2,1,0:T(8,128)}, u32[]{:S(2)}) copy-start(f32[2,16,128]{2,1,0:T(8,128)} %get-tuple-element.377) | copy-start | bytes 49156 | tf_op jit(solution)/shard_map/while
  311.9 8.9 %copy-start.12 = (f32[32]{0:T(128)S(1)}, f32[32]{0:T(128)}, u32[]{:S(2)}) copy-start(f32[32]{0:T(128)} %copy-done.11) | copy-start | bytes 388 | tf_op jit(solution)/shard_map/while
  320.8 6.7 %copy-start.2 = (bf16[128,128]{1,0:T(8,128)(2,1)}, bf16[128,128]{1,0:T(8,128)(2,1)S(1)}, u32[]{:S(2)}) copy-start(bf16[128,128]{1,0:T(8,128)(2,1)S(1)} %get-tuple-element.396) | copy-start | bytes 98308 | tf_op jit(solution)/shard_map/while
  347.1 4.5 %copy-start.5 = (f32[8,16,128]{2,1,0:T(8,128)S(1)}, f32[8,16,128]{2,1,0:T(8,128)}, u32[]{:S(2)}) copy-start(f32[8,16,128]{2,1,0:T(8,128)} %fusion.408) | copy-start | bytes 196612 | tf_op jit(solution)/shard_map/while
  371.9 4.5 %copy-start.3 = (bf16[128,128]{1,0:T(8,128)(2,1)S(1)}, bf16[128,128]{1,0:T(8,128)(2,1)}, u32[]{:S(2)}) copy-start(bf16[128,128]{1,0:T(8,128)(2,1)} %copy-done.2) | copy-start | bytes 98308 | tf_op jit(solution)/shard_map/while
  371.9 4.5 %copy-start.4 = (f32[8,16,128]{2,1,0:T(8,128)S(1)}, f32[8,16,128]{2,1,0:T(8,128)}, u32[]{:S(2)}) copy-start(f32[8,16,128]{2,1,0:T(8,128)} %fusion.422) | copy-start | bytes 196612 | tf_op jit(solution)/shard_map/while
  374.2 8.3 %copy-start.6 = (f32[2,16,128]{2,1,0:T(8,128)S(1)}, f32[2,16,128]{2,1,0:T(8,128)}, u32[]{:S(2)}) copy-start(f32[2,16,128]{2,1,0:T(8,128)} %get-tuple-element.377) | copy-start | bytes 49156 | tf_op jit(solution)/shard_map/while
  374.2 8.9 %copy-start.12 = (f32[32]{0:T(128)S(1)}, f32[32]{0:T(128)}, u32[]{:S(2)}) copy-start(f32[32]{0:T(128)} %copy-done.11) | copy-start | bytes 388 | tf_op jit(solution)/shard_map/while
  383.1 34.5 %copy-start.1 = (bf16[2,2,32,16,128]{4,3,2,1,0:T(8,128)(2,1)S(1)}, bf16[2,2,32,16,128]{4,3,2,1,0:T(8,128)(2,1)}, u32[]{:S(2)}) copy-start(bf16[2,2,32,16,128]{4,3,2,1,0:T(8,128)(2,1)} %param.10) | copy-start | bytes 1572868
  383.1 2.8 collective-permute-start
  386.6 4.1 collective-permute-start.1
  390.7 2.9 collective-permute-start.2
  393.6 4.1 collective-permute-start.3
  (11 other events, 9.1 us)
Sparse Core Ops, SparseCore 0:
  10.7 39.3 all-gather.1
